TPU v7x, 256 devices: a whole 4x4x8 slice. The times are simulated.
256 devices in a mesh: lon: 8 (over z), lat: 8 (over x, y_hi), dp: 4 (over y_lo, core).
Axes of the slice: x: 4, y: 4 (y_hi: 2, y_lo: 2; y = y_hi * 2 + y_lo), z: 8, core: 2. Of those that a mesh axis runs over, the one named last changes fastest.
Arguments:
- fields: bfloat16 [4, 256, 64, 1024], P('dp', None, 'lat', 'lon'), may hold values from -6 to 6
- weight_one: bfloat16 [9, 256, 256], replicated, may hold values from -0.125 to 0.125
- weight_two: bfloat16 [9, 256, 256], replicated, may hold values from -0.125 to 0.125
- edge_flips: int32 [7, 8], replicated, may hold values from 0 to 1, as said below
- cotangent: bfloat16 [4, 256, 64, 1024], P('dp', None, 'lat', 'lon'), may hold values from -6 to 6
Outputs:
- output: bfloat16 [4, 256, 64, 1024], P('dp', None, 'lat', 'lon')
- grad_fields: bfloat16 [4, 256, 64, 1024], P('dp', None, 'lat', 'lon')
- grad_one: float32 [9, 256, 256], replicated
- grad_two: float32 [9, 256, 256], replicated
Inputs may be any that keep to these rules, and one draw needn't show every extreme that they name: `edge_flips`: 0 on every edge inside a face; only row 8 // 2 - 1, the boundary between the band's two face rows, may hold 1, where the two faces meeting at that longitude tile store longitude in opposite orders.
All inputs are finite; a program needn't handle non-finite values.
Results may differ from a plain program's by a relative error of at most 0.0034.
Values may be sent and summed in bfloat16 or wider, within the bound.
No kernel may reach another device: no remote copies, remote signals or barrier semaphores. Data moves between devices by JAX's collectives and lax.ppermute only.
A program may use at most 128 MiB of HBM per device.

v0:
```python
import jax
import jax.numpy as jnp
from jax import lax
from jax.sharding import PartitionSpec as P


def with_halo(cells, sides, width, closed):
    for axis, dim in sides:
        count = lax.axis_size(axis)
        ends = count if closed else count - 1
        head = lax.slice_in_dim(cells, 0, width, axis=dim)
        tail = lax.slice_in_dim(cells, cells.shape[dim] - width, cells.shape[dim], axis=dim)
        cells = jnp.concatenate(
            [
                lax.ppermute(tail, axis, [(i, (i + 1) % count) for i in range(ends)]),
                cells,
                lax.ppermute(head, axis, [((i + 1) % count, i) for i in range(ends)]),
            ],
            axis=dim,
        )
    return cells


def oriented(line_cells, reverse_flag):
    return jnp.where(reverse_flag == 1, jnp.flip(line_cells, -1), line_cells)


def edge_flags(edge_flips):
    lat_index = lax.axis_index("lat")
    lon_index = lax.axis_index("lon")
    lat_count = lax.axis_size("lat")
    upper_flip = lax.dynamic_slice(edge_flips, (jnp.maximum(lat_index - 1, 0), lon_index), (1, 1))[
        0, 0
    ]
    lower_flip = lax.dynamic_slice(
        edge_flips, (jnp.minimum(lat_index, lat_count - 2), lon_index), (1, 1)
    )[0, 0]
    return (upper_flip, lower_flip, lat_index > 0, lat_index < lat_count - 1)


def padded(source, edge_info):
    upper_flip, lower_flip, has_upper, has_lower = edge_info
    extended = with_halo(source, (("lon", 3), ("lat", 2)), 1, True)
    top_rim = jnp.where(has_upper, extended[:, :, 0, :], jnp.zeros_like(extended[:, :, 0, :]))
    bottom = jnp.where(has_lower, extended[:, :, -1, :], jnp.zeros_like(extended[:, :, -1, :]))
    top_rim = oriented(top_rim, upper_flip)
    bottom = oriented(bottom, lower_flip)
    return jnp.concatenate(
        [top_rim[:, :, None, :], extended[:, :, 1:-1, :], bottom[:, :, None, :]], 2
    )


def patches_of(padded_in, tile_rows, tile_cols):
    return jnp.stack(
        [
            padded_in[:, :, tap_row : tap_row + tile_rows, tap_col : tap_col + tile_cols]
            for tap_row in range(3)
            for tap_col in range(3)
        ],
        1,
    )


def convolve(patches, weight):
    return jnp.einsum("toc,btchw->bohw", weight, patches, preferred_element_type=jnp.float32)


def transposed(grad_tile, weight, tile_rows, tile_cols):
    batch, chans = (grad_tile.shape[0], weight.shape[2])
    padded_grad = jnp.zeros((batch, chans, tile_rows + 2, tile_cols + 2), jnp.float32)
    for tap_row in range(3):
        for tap_col in range(3):
            tap_term = jnp.einsum(
                "oc,bohw->bchw",
                weight[3 * tap_row + tap_col],
                grad_tile,
                preferred_element_type=jnp.float32,
            )
            padded_grad = padded_grad.at[
                :, :, tap_row : tap_row + tile_rows, tap_col : tap_col + tile_cols
            ].add(tap_term)
    return padded_grad


def returned(padded_grad, edge_info):
    upper_flip, lower_flip, has_upper, has_lower = edge_info
    top_rim = oriented(padded_grad[:, :, 0, :], upper_flip)
    bottom = oriented(padded_grad[:, :, -1, :], lower_flip)
    rim_rows = jnp.stack([top_rim, bottom], 2)
    received = with_halo(rim_rows, (("lat", 2),), 1, False)
    interior = padded_grad[:, :, 1:-1, :]
    interior = interior.at[:, :, 0, :].add(received[:, :, 0, :])
    interior = interior.at[:, :, -1, :].add(received[:, :, -1, :])
    side_cols = jnp.stack([interior[..., 0], interior[..., -1]], -1)
    beside = with_halo(side_cols, (("lon", 3),), 1, True)
    result = interior[..., 1:-1]
    result = result.at[..., 0].add(beside[..., 0])
    result = result.at[..., -1].add(beside[..., -1])
    return result


def per_device(fields, weight_one, weight_two, edge_flips, cotangent):
    tile_rows, tile_cols = (fields.shape[2], fields.shape[3])
    edge_info = edge_flags(edge_flips)
    patch_in = patches_of(padded(fields, edge_info), tile_rows, tile_cols)
    hidden = convolve(patch_in, weight_one)
    activation = jax.nn.silu(hidden).astype(jnp.bfloat16)
    patch_act = patches_of(padded(activation, edge_info), tile_rows, tile_cols)
    output = (fields.astype(jnp.float32) + convolve(patch_act, weight_two)).astype(jnp.bfloat16)
    local_two = jnp.einsum(
        "bohw,btchw->toc", cotangent, patch_act, preferred_element_type=jnp.float32
    )
    back_act = returned(transposed(cotangent, weight_two, tile_rows, tile_cols), edge_info)
    sigmoid_h = jax.nn.sigmoid(hidden)
    back_hidden = (back_act * sigmoid_h * (1.0 + hidden * (1.0 - sigmoid_h))).astype(jnp.bfloat16)
    local_one = jnp.einsum(
        "bohw,btchw->toc", back_hidden, patch_in, preferred_element_type=jnp.float32
    )
    grad_one, grad_two = lax.psum((local_one, local_two), ("lon", "lat", "dp"))
    back_fields = returned(transposed(back_hidden, weight_one, tile_rows, tile_cols), edge_info)
    grad_fields = (cotangent.astype(jnp.float32) + back_fields).astype(jnp.bfloat16)
    return (output, grad_fields, grad_one, grad_two)


def solution(mesh):
    in_specs = (P("dp", None, "lat", "lon"), P(), P(), P(), P("dp", None, "lat", "lon"))
    out_specs = (P("dp", None, "lat", "lon"), P("dp", None, "lat", "lon"), P(), P())
    return jax.shard_map(
        per_device, mesh=mesh, in_specs=in_specs, out_specs=out_specs, check_vma=False
    )
```

profile of v0, /device:TPU:97, one launch (start us, length us, event | category | flops | bytes accessed | tf_op | source)
XLA Modules:
  0.0 453.6 jit_solution(17974031605681476931)
XLA Ops:
  8.6 2.9 collective-permute-start
  15.6 2.5 fusion.20
  18.1 4.0 scatter-add.89
  22.1 3.2 add_select_fusion.1
  25.3 4.0 scatter-add.90
  31.9 2.7 scatter-add.94
  35.9 2.7 scatter-add.95
  41.1 2.7 scatter-add.99
  45.1 2.7 scatter-add.100
  51.2 5.2 %collective-permute-start.3 = (bf16[1,256,1,130]{1,3,2,0:T(8,128)(2,1)S(1)}, bf16[1,256,1,130]{1,3,2,0:T(8,128)(2,1)S(1)}, u32[]{:S(2)}, u32[]{:S(2)}) collective-permute-start(bf16[1,256,1,130]{1,3,2,0:T(8,128)(2,1)S(1)} %get-tuple-element.342), channel_id=1, source_target_pairs={{4,0},{8,4},{12,8},{16,12},{20,16},{24,20},{28,24},{0,28},{5,1},{9... | collective-permute-start | bytes 199688 | tf_op jit(solution)/shard_map/ppermute | solution.py:17
  57.8 5.5 %collective-permute-start.8 = (f32[1,256,1,130]{1,3,2,0:T(8,128)S(1)}, f32[1,256,1,130]{1,3,2,0:T(8,128)S(1)}, u32[]{:S(2)}, u32[]{:S(2)}) collective-permute-start(f32[1,256,1,130]{1,3,2,0:T(8,128)S(1)} %get-tuple-element.327), channel_id=1, source_target_pairs={{0,4},{4,8},{8,12},{12,16},{16,20},{20,24},{24,28},{1,5},{5,9},{9,... | collective-permute-start | bytes 399368 | tf_op jit(solution)/shard_map/ppermute | solution.py:15
  64.7 6.4 %collective-permute-done.2 = bf16[1,256,1,130]{1,3,2,0:T(8,128)(2,1)S(1)} collective-permute-done((bf16[1,256,1,130]{1,3,2,0:T(8,128)(2,1)S(1)}, bf16[1,256,1,130]{1,3,2,0:T(8,128)(2,1)S(1)}, u32[]{:S(2)}, u32[]{:S(2)}) %collective-permute-start.2) | collective-permute-done | bytes 66592 | tf_op jit(solution)/shard_map/ppermute | solution.py:15
  73.6 2.7 collective-permute-start.10
  85.7 4.4 multiply_convert_fusion
  90.1 2.9 fusion.8
  93.3 2.6 fusion.29
  97.6 7.2 %scatter-add.110 = f32[1,256,10,130]{1,3,2,0:T(8,128)S(1)} dynamic-update-slice(f32[1,256,10,130]{1,3,2,0:T(8,128)S(1)} %scatter-add.109, f32[1,256,8,128]{1,3,2,0:T(8,128)} %fusion.29, s32[]{:T(128)} %constant.657.clone.1, s32[]{:T(128)} %constant.657.clone.1, s32[]{:T(128)} %bitcast.51, s32[]{:T(128)} %bitcast.52) | dynamic-update-slice | bytes 2097156 | tf_op jit(solution)/shard_map/scatter-add | solution.py:81
  104.8 4.1 add_select_fusion
  108.9 7.2 %scatter-add.111 = f32[1,256,10,130]{1,3,2,0:T(8,128)S(1)} dynamic-update-slice(f32[1,256,10,130]{1,3,2,0:T(8,128)S(1)} %scatter-add.110, f32[1,256,8,128]{1,3,2,0:T(8,128)} %add_select_fusion, s32[]{:T(128)} %constant.657.clone.1, s32[]{:T(128)} %constant.657.clone.1, s32[]{:T(128)} %bitcast.57, s32[]{:T(128)} %bitcast.58) | dynamic-update-slice | bytes 2097156 | tf_op jit(solution)/shard_map/scatter-add | solution.py:81
  119.5 5.9 %scatter-add.115 = f32[1,256,10,130]{1,3,2,0:T(8,128)S(1)} dynamic-update-slice(f32[1,256,10,130]{1,3,2,0:T(8,128)S(1)} %fusion.31, f32[1,256,8,128]{1,3,2,0:T(8,128)} %fusion.32, s32[]{:T(128)} %constant.657.clone.1, s32[]{:T(128)} %constant.657.clone.1, s32[]{:T(128)} %constant.670.clone.1, s32[]{:T(128)} %constant.670.clone.1) | dynamic-update-slice | bytes 2097156 | tf_op jit(solution)/shard_map/scatter-add | solution.py:81
  127.6 5.9 %scatter-add.116 = f32[1,256,10,130]{1,3,2,0:T(8,128)S(1)} dynamic-update-slice(f32[1,256,10,130]{1,3,2,0:T(8,128)S(1)} %scatter-add.115, f32[1,256,8,128]{1,3,2,0:T(8,128)} %fusion.33, s32[]{:T(128)} %constant.657.clone.1, s32[]{:T(128)} %constant.657.clone.1, s32[]{:T(128)} %constant.670.clone.1, s32[]{:T(128)} %constant.667.clone.1) | dynamic-update-slice | bytes 2097156 | tf_op jit(solution)/shard_map/scatter-add | solution.py:81
  136.8 5.9 %scatter-add.120 = f32[1,256,10,130]{1,3,2,0:T(8,128)S(1)} dynamic-update-slice(f32[1,256,10,130]{1,3,2,0:T(8,128)S(1)} %fusion.35, f32[1,256,8,128]{1,3,2,0:T(8,128)} %fusion.36, s32[]{:T(128)} %constant.657.clone.1, s32[]{:T(128)} %constant.657.clone.1, s32[]{:T(128)} %constant.667.clone.1, s32[]{:T(128)} %constant.670.clone.1) | dynamic-update-slice | bytes 2097156 | tf_op jit(solution)/shard_map/scatter-add | solution.py:81
  145.6 5.9 %scatter-add.121 = f32[1,256,10,130]{1,3,2,0:T(8,128)S(1)} dynamic-update-slice(f32[1,256,10,130]{1,3,2,0:T(8,128)S(1)} %scatter-add.120, f32[1,256,8,128]{1,3,2,0:T(8,128)} %fusion.37, s32[]{:T(128)} %constant.657.clone.1, s32[]{:T(128)} %constant.657.clone.1, s32[]{:T(128)} %constant.667.clone.1, s32[]{:T(128)} %constant.667.clone.1) | dynamic-update-slice | bytes 2097156 | tf_op jit(solution)/shard_map/scatter-add | solution.py:81
  151.5 3.0 collective-permute-start.6
  155.7 2.6 collective-permute-done.6
  162.9 2.9 fusion.11
  166.5 3.0 collective-permute-start.12
  171.4 6.0 %collective-permute-done.13 = f32[1,256,1,130]{1,3,2,0:T(8,128)S(1)} collective-permute-done((f32[1,256,1,130]{1,3,2,0:T(8,128)S(1)}, f32[1,256,1,130]{1,3,2,0:T(8,128)S(1)}, u32[]{:S(2)}, u32[]{:S(2)}) %collective-permute-start.13) | collective-permute-done | bytes 133152 | tf_op jit(solution)/shard_map/ppermute | solution.py:17
  180.2 3.8 fusion.41
  185.4 3.6 collective-permute-done.15
  190.3 251.3 %all-reduce.5.cloned.1.call-done = (f32[9,256,256]{1,2,0:T(8,128)}, f32[9,256,256]{1,2,0:T(8,128)}) async-done(((f32[9,256,256]{1,2,0:T(8,128)}, f32[9,256,256]{1,2,0:T(8,128)}), (f32[9,256,256]{1,2,0:T(8,128)}, f32[9,256,256]{1,2,0:T(8,128)})) %all-reduce.5.cloned.1.call-update) | async-done | bytes 4718608 | tf_op jit(solution)/shard_map/psum | solution.py:119
  441.6 3.2 copy.38
  (136 shorter events, 58.9 us)
Async XLA Ops:
  7.2 7.0 %copy-start = (bf16[1,256,8,128]{3,2,1,0:T(8,128)(2,1)S(1)}, bf16[1,256,8,128]{3,2,1,0:T(8,128)(2,1)}, u32[]{:S(2)}) copy-start(bf16[1,256,8,128]{3,2,1,0:T(8,128)(2,1)} %param.61) | copy-start | bytes 1572868
  7.2 434.4 %all-reduce.5.cloned.1.call-start = ((), (), s32[]{:S(2)}) async-start(), calls=%async_computation | async-start | bytes 9437184 | tf_op jit(solution)/shard_map/psum | solution.py:119
  8.6 42.5 %collective-permute-start = (bf16[1,256,8,1]{1,3,2,0:T(2,128)(2,1)S(1)}, bf16[1,256,8,1]{1,3,2,0:T(2,128)(2,1)S(1)}, u32[]{:S(2)}, u32[]{:S(2)}) collective-permute-start(bf16[1,256,8,1]{1,3,2,0:T(2,128)(2,1)S(1)} %get-tuple-element.346), channel_id=1, source_target_pairs={{0,32},{32,64},{64,96},{96,128},{128,160},{160,192},{192,224},{224... | collective-permute-start | bytes 12296 | tf_op jit(solution)/shard_map/ppermute | solution.py:15
  11.5 39.6 %collective-permute-start.1 = (bf16[1,256,8,1]{1,3,2,0:T(2,128)(2,1)S(1)}, bf16[1,256,8,1]{1,3,2,0:T(2,128)(2,1)S(1)}, u32[]{:S(2)}, u32[]{:S(2)}) collective-permute-start(bf16[1,256,8,1]{1,3,2,0:T(2,128)(2,1)S(1)} %get-tuple-element.347), channel_id=1, source_target_pairs={{32,0},{64,32},{96,64},{128,96},{160,128},{192,160},{224,192},{0,2... | collective-permute-start | bytes 12296 | tf_op jit(solution)/shard_map/ppermute | solution.py:17
  51.2 13.1 %collective-permute-start.3 = (bf16[1,256,1,130]{1,3,2,0:T(8,128)(2,1)S(1)}, bf16[1,256,1,130]{1,3,2,0:T(8,128)(2,1)S(1)}, u32[]{:S(2)}, u32[]{:S(2)}) collective-permute-start(bf16[1,256,1,130]{1,3,2,0:T(8,128)(2,1)S(1)} %get-tuple-element.342), channel_id=1, source_target_pairs={{4,0},{8,4},{12,8},{16,12},{20,16},{24,20},{28,24},{0,28},{5,1},{9... | collective-permute-start | bytes 199688 | tf_op jit(solution)/shard_map/ppermute | solution.py:17
  56.5 17.0 %collective-permute-start.9 = (f32[1,256,1,130]{1,3,2,0:T(8,128)S(1)}, f32[1,256,1,130]{1,3,2,0:T(8,128)S(1)}, u32[]{:S(2)}, u32[]{:S(2)}) collective-permute-start(f32[1,256,1,130]{1,3,2,0:T(8,128)S(1)} %get-tuple-element.326), channel_id=1, source_target_pairs={{4,0},{8,4},{12,8},{16,12},{20,16},{24,20},{28,24},{5,1},{9,5},{13... | collective-permute-start | bytes 399368 | tf_op jit(solution)/shard_map/ppermute | solution.py:17
  57.8 14.8 %collective-permute-start.8 = (f32[1,256,1,130]{1,3,2,0:T(8,128)S(1)}, f32[1,256,1,130]{1,3,2,0:T(8,128)S(1)}, u32[]{:S(2)}, u32[]{:S(2)}) collective-permute-start(f32[1,256,1,130]{1,3,2,0:T(8,128)S(1)} %get-tuple-element.327), channel_id=1, source_target_pairs={{0,4},{4,8},{8,12},{12,16},{16,20},{20,24},{24,28},{1,5},{5,9},{9,... | collective-permute-start | bytes 399368 | tf_op jit(solution)/shard_map/ppermute | solution.py:15
  64.3 6.8 %collective-permute-start.2 = (bf16[1,256,1,130]{1,3,2,0:T(8,128)(2,1)S(1)}, bf16[1,256,1,130]{1,3,2,0:T(8,128)(2,1)S(1)}, u32[]{:S(2)}, u32[]{:S(2)}) collective-permute-start(bf16[1,256,1,130]{1,3,2,0:T(8,128)(2,1)S(1)} %get-tuple-element.343), channel_id=1, source_target_pairs={{0,4},{4,8},{8,12},{12,16},{16,20},{20,24},{24,28},{28,0},{1,5},{5... | collective-permute-start | bytes 199688 | tf_op jit(solution)/shard_map/ppermute | solution.py:15
  72.2 1.3 copy-start.1
  73.6 12.2 %copy-start.5 = (bf16[9,256,256]{2,1,0:T(8,128)(2,1)S(1)}, bf16[9,256,256]{2,1,0:T(8,128)(2,1)}, u32[]{:S(2)}) copy-start(bf16[9,256,256]{2,1,0:T(8,128)(2,1)} %param.58) | copy-start | bytes 3538948
  73.6 6.1 %collective-permute-start.10 = (f32[1,256,8,1]{1,3,2,0:T(1,128)S(1)}, f32[1,256,8,1]{1,3,2,0:T(1,128)S(1)}, u32[]{:S(2)}, u32[]{:S(2)}) collective-permute-start(f32[1,256,8,1]{1,3,2,0:T(1,128)S(1)} %get-tuple-element.333), channel_id=1, source_target_pairs={{0,32},{32,64},{64,96},{96,128},{128,160},{160,192},{192,224},{224... | collective-permute-start | bytes 24584 | tf_op jit(solution)/shard_map/ppermute | solution.py:15
  76.4 2.1 copy-start.8
  79.7 3.7 collective-permute-start.11
  85.7 4.4 copy-start.9
  96.0 46.7 %collective-permute-start.4 = (bf16[1,256,8,1]{1,3,2,0:T(2,128)(2,1)S(1)}, bf16[1,256,8,1]{1,3,2,0:T(2,128)(2,1)S(1)}, u32[]{:S(2)}, u32[]{:S(2)}) collective-permute-start(bf16[1,256,8,1]{1,3,2,0:T(2,128)(2,1)S(1)} %get-tuple-element.344), channel_id=1, source_target_pairs={{0,32},{32,64},{64,96},{96,128},{128,160},{160,192},{192,224},{224... | collective-permute-start | bytes 12296 | tf_op jit(solution)/shard_map/ppermute | solution.py:15
  96.6 46.1 %collective-permute-start.5 = (bf16[1,256,8,1]{1,3,2,0:T(2,128)(2,1)S(1)}, bf16[1,256,8,1]{1,3,2,0:T(2,128)(2,1)S(1)}, u32[]{:S(2)}, u32[]{:S(2)}) collective-permute-start(bf16[1,256,8,1]{1,3,2,0:T(2,128)(2,1)S(1)} %get-tuple-element.345), channel_id=1, source_target_pairs={{32,0},{64,32},{96,64},{128,96},{160,128},{192,160},{224,192},{0,2... | collective-permute-start | bytes 12296 | tf_op jit(solution)/shard_map/ppermute | solution.py:17
  143.4 11.1 %collective-permute-start.7 = (bf16[1,256,1,130]{1,3,2,0:T(8,128)(2,1)}, bf16[1,256,1,130]{1,3,2,0:T(8,128)(2,1)}, u32[]{:S(2)}, u32[]{:S(2)}) collective-permute-start(bf16[1,256,1,130]{1,3,2,0:T(8,128)(2,1)} %get-tuple-element.338), channel_id=1, source_target_pairs={{4,0},{8,4},{12,8},{16,12},{20,16},{24,20},{28,24},{0,28},{5,1},{9... | collective-permute-start | bytes 199688 | tf_op jit(solution)/shard_map/ppermute | solution.py:17
  145.6 5.9 %copy-start.7 = (bf16[1,256,1,130]{1,3,2,0:T(8,128)(2,1)S(1)}, bf16[1,256,1,130]{1,3,2,0:T(8,128)(2,1)}, u32[]{:S(2)}) copy-start(bf16[1,256,1,130]{1,3,2,0:T(8,128)(2,1)} %get-tuple-element.339) | copy-start | bytes 199684
  151.5 6.9 %collective-permute-start.6 = (bf16[1,256,1,130]{1,3,2,0:T(8,128)(2,1)S(1)}, bf16[1,256,1,130]{1,3,2,0:T(8,128)(2,1)S(1)}, u32[]{:S(2)}, u32[]{:S(2)}) collective-permute-start(bf16[1,256,1,130]{1,3,2,0:T(8,128)(2,1)S(1)} %copy-done.7), channel_id=1, source_target_pairs={{0,4},{4,8},{8,12},{12,16},{16,20},{20,24},{24,28},{28,0},{1,5},{5... | collective-permute-start | bytes 199688 | tf_op jit(solution)/shard_map/ppermute | solution.py:15
  160.8 2.1 copy-start.10
  166.5 4.9 %collective-permute-start.12 = (f32[1,256,1,130]{1,3,2,0:T(8,128)S(1)}, f32[1,256,1,130]{1,3,2,0:T(8,128)S(1)}, u32[]{:S(2)}, u32[]{:S(2)}) collective-permute-start(f32[1,256,1,130]{1,3,2,0:T(8,128)S(1)} %get-tuple-element.323), channel_id=1, source_target_pairs={{0,4},{4,8},{8,12},{12,16},{16,20},{20,24},{24,28},{1,5},{5,9},{9,... | collective-permute-start | bytes 399368 | tf_op jit(solution)/shard_map/ppermute | solution.py:15
  169.8 10.4 %copy-start.6 = (bf16[9,256,256]{2,1,0:T(8,128)(2,1)S(1)}, bf16[9,256,256]{2,1,0:T(8,128)(2,1)}, u32[]{:S(2)}) copy-start(bf16[9,256,256]{2,1,0:T(8,128)(2,1)} %param.59) | copy-start | bytes 3538948
  169.9 7.4 %collective-permute-start.13 = (f32[1,256,1,130]{1,3,2,0:T(8,128)S(1)}, f32[1,256,1,130]{1,3,2,0:T(8,128)S(1)}, u32[]{:S(2)}, u32[]{:S(2)}) collective-permute-start(f32[1,256,1,130]{1,3,2,0:T(8,128)S(1)} %get-tuple-element.322), channel_id=1, source_target_pairs={{4,0},{8,4},{12,8},{16,12},{20,16},{24,20},{28,24},{5,1},{9,5},{13... | collective-permute-start | bytes 399368 | tf_op jit(solution)/shard_map/ppermute | solution.py:17
  177.4 1.0 copy-start.2
  178.4 6.9 %collective-permute-start.14 = (f32[1,256,8,1]{1,3,2,0:T(1,128)S(1)}, f32[1,256,8,1]{1,3,2,0:T(1,128)S(1)}, u32[]{:S(2)}, u32[]{:S(2)}) collective-permute-start(f32[1,256,8,1]{1,3,2,0:T(1,128)S(1)} %get-tuple-element.331), channel_id=1, source_target_pairs={{0,32},{32,64},{64,96},{96,128},{128,160},{160,192},{192,224},{224... | collective-permute-start | bytes 24584 | tf_op jit(solution)/shard_map/ppermute | solution.py:15
  180.2 4.9 %copy-start.3 = (f32[1,256,8,130]{1,3,2,0:T(8,128)S(1)}, f32[1,256,8,130]{1,3,2,0:T(8,128)}, u32[]{:S(2)}) copy-start(f32[1,256,8,130]{1,3,2,0:T(8,128)} %copy-done.2) | copy-start | bytes 3194884
  185.2 3.8 collective-permute-start.15
  441.6 3.2 copy-start.4
Sparse Core Ops, SparseCore 0:
  165.9 275.6 all-reduce.4
where the time goes:
time: 455 us; the launch traced here: 454 us
  waiting for transfers between devices  272 us (60%)
  local copies, waits for them, and re-layouts  84.1 us (18%)
  matrix products  46.6 us (10%)
  starting transfers between devices  28.6 us (6%)
  between operations  16.1 us (4%)
  other arithmetic  6.15 us (1%)
    psum x1, waiting for transfers between devices, per_device(): grad_one, grad_two = lax.psum((local_one, local_two), ('lon', 'lat', 'dp'))  251 us
    scatter-add x14, local copies, waits for them, and re-layouts, transposed(): padded_grad = padded_grad.at[:, :, tap_row:tap_row + tile_rows, tap_col:t...  57 us
    dot_general x18, matrix products, transposed(): jnp.einsum('oc,bohw->bchw', weight[3 * tap_row + tap_col], grad_tile, pre...  32.6 us
    ppermute x8, starting transfers between devices, with_halo(): lax.ppermute(tail, axis, [(i, (i + 1) % count) for i in range(ends)])  19.6 us
    unnamed x40, local copies, waits for them, and re-layouts  16.1 us
    ppermute x8, waiting for transfers between devices, with_halo(): lax.ppermute(head, axis, [((i + 1) % count, i) for i in range(ends)])  11.8 us
  transfers between devices with their start and end apart: 17, of which 6 were waited for; matrix products, arithmetic and copies ran while one was open for 23% of the time, Pallas kernels for 0%

commit v1 on v0

--- a/solution.py
+++ b/solution.py
@@ -116,7 +116,7 @@
     local_one = jnp.einsum(
         "bohw,btchw->toc", back_hidden, patch_in, preferred_element_type=jnp.float32
     )
-    grad_one, grad_two = lax.psum((local_one, local_two), ("lon", "lat", "dp"))
+    grad_one, grad_two = lax.psum(lax.psum((local_one, local_two), "lon"), ("lat", "dp"))
     back_fields = returned(transposed(back_hidden, weight_one, tile_rows, tile_cols), edge_info)
     grad_fields = (cotangent.astype(jnp.float32) + back_fields).astype(jnp.bfloat16)
     return (output, grad_fields, grad_one, grad_two)

time: 455 us -> 375 us (0.82)
  waiting for transfers between devices: 272 us -> 186 us
    psum x1 -> x2, waiting for transfers between devices: 251 us -> 162 us  [the longest x1 99.3 us: per_device(): lax.psum(lax.psum((local_one, local_two), 'lon'), ('lat', 'dp'))]
    unnamed x40 -> x46, local copies, waits for them, and re-layouts: 16.1 us -> 16.6 us
  transfers between devices with their start and end apart: 17 -> 18, of which waited for: 6 -> 10; matrix products, arithmetic and copies ran while one was open for 23% -> 30% of each run, Pallas kernels for 0% -> 0%
where the time goes in v1:
time: 375 us; the launch traced here: 371 us
  waiting for transfers between devices  186 us (50%)
  local copies, waits for them, and re-layouts  85.5 us (23%)
  matrix products  47.3 us (13%)
  starting transfers between devices  30.3 us (8%)
  between operations  16.1 us (4%)
  other arithmetic  6.47 us (2%)
    psum x1, waiting for transfers between devices, per_device(): lax.psum(lax.psum((local_one, local_two), 'lon'), ('lat', 'dp'))  99.3 us
    psum x1, waiting for transfers between devices, per_device(): lax.psum((local_one, local_two), 'lon')  62.5 us
    scatter-add x14, local copies, waits for them, and re-layouts, transposed(): padded_grad = padded_grad.at[:, :, tap_row:tap_row + tile_rows, tap_col:t...  56.7 us
    dot_general x18, matrix products, transposed(): jnp.einsum('oc,bohw->bchw', weight[3 * tap_row + tap_col], grad_tile, pre...  33.3 us
    ppermute x8, starting transfers between devices, with_halo(): lax.ppermute(tail, axis, [(i, (i + 1) % count) for i in range(ends)])  20 us
    unnamed x46, local copies, waits for them, and re-layouts  16.6 us
    ppermute x8, waiting for transfers between devices, with_halo(): lax.ppermute(head, axis, [((i + 1) % count, i) for i in range(ends)])  12.3 us
    ppermute x8, waiting for transfers between devices, with_halo(): lax.ppermute(tail, axis, [(i, (i + 1) % count) for i in range(ends)])  11.5 us
  transfers between devices with their start and end apart: 18, of which 10 were waited for; matrix products, arithmetic and copies ran while one was open for 30% of the time, Pallas kernels for 0%

profile of v1, /device:TPU:97, one launch (start us, length us, event | category | flops | bytes accessed | tf_op | source)
XLA Modules:
  0.0 371.2 jit_solution(3184082240792568851)
XLA Ops:
  8.6 2.9 collective-permute-start
  18.0 3.9 %scatter-add.89 = f32[1,256,10,130]{1,3,2,0:T(8,128)S(1)} dynamic-update-slice(f32[1,256,10,130]{1,3,2,0:T(8,128)S(1)} %scatter-add.86, f32[1,256,8,128]{1,3,2,0:T(8,128)S(1)} %fusion.20, s32[]{:T(128)} %constant.657.clone.1, s32[]{:T(128)} %constant.657.clone.1, s32[]{:T(128)} %bitcast.51, s32[]{:T(128)} %bitcast.52) | dynamic-update-slice | bytes 2097156 | tf_op jit(solution)/shard_map/scatter-add | solution.py:81
  21.9 3.2 add_select_fusion.1
  25.1 4.0 %scatter-add.90 = f32[1,256,10,130]{1,3,2,0:T(8,128)S(1)} dynamic-update-slice(f32[1,256,10,130]{1,3,2,0:T(8,128)S(1)} %scatter-add.89, f32[1,256,8,128]{1,3,2,0:T(8,128)S(1)} %add_select_fusion.1, s32[]{:T(128)} %constant.657.clone.1, s32[]{:T(128)} %constant.657.clone.1, s32[]{:T(128)} %bitcast.57, s32[]{:T(128)} %bitcast.58) | dynamic-update-slice | bytes 2097156 | tf_op jit(solution)/shard_map/scatter-add | solution.py:81
  31.6 2.7 scatter-add.94
  35.6 2.7 scatter-add.95
  40.9 2.7 scatter-add.99
  44.9 2.7 scatter-add.100
  50.9 5.2 %collective-permute-start.3 = (bf16[1,256,1,130]{1,3,2,0:T(8,128)(2,1)S(1)}, bf16[1,256,1,130]{1,3,2,0:T(8,128)(2,1)S(1)}, u32[]{:S(2)}, u32[]{:S(2)}) collective-permute-start(bf16[1,256,1,130]{1,3,2,0:T(8,128)(2,1)S(1)} %get-tuple-element.344), channel_id=1, source_target_pairs={{4,0},{8,4},{12,8},{16,12},{20,16},{24,20},{28,24},{0,28},{5,1},{9... | collective-permute-start | bytes 199688 | tf_op jit(solution)/shard_map/ppermute | solution.py:17
  57.5 5.5 %collective-permute-start.8 = (f32[1,256,1,130]{1,3,2,0:T(8,128)S(1)}, f32[1,256,1,130]{1,3,2,0:T(8,128)S(1)}, u32[]{:S(2)}, u32[]{:S(2)}) collective-permute-start(f32[1,256,1,130]{1,3,2,0:T(8,128)S(1)} %get-tuple-element.329), channel_id=1, source_target_pairs={{0,4},{4,8},{8,12},{12,16},{16,20},{20,24},{24,28},{1,5},{5,9},{9,... | collective-permute-start | bytes 399368 | tf_op jit(solution)/shard_map/ppermute | solution.py:15
  64.4 6.4 %collective-permute-done.2 = bf16[1,256,1,130]{1,3,2,0:T(8,128)(2,1)S(1)} collective-permute-done((bf16[1,256,1,130]{1,3,2,0:T(8,128)(2,1)S(1)}, bf16[1,256,1,130]{1,3,2,0:T(8,128)(2,1)S(1)}, u32[]{:S(2)}, u32[]{:S(2)}) %collective-permute-start.2) | collective-permute-done | bytes 66592 | tf_op jit(solution)/shard_map/ppermute | solution.py:15
  73.3 2.7 collective-permute-start.10
  85.5 4.4 %multiply_convert_fusion = (bf16[1,256,8,128]{1,3,2,0:T(8,128)(2,1)S(1)}, bf16[1,256,8,128]{1,3,2,0:T(8,128)(2,1)S(1)}) fusion(f32[1,256,8,128]{1,3,2,0:T(8,128)} %scatter-add.106, bf16[9,256,256]{2,1,0:T(8,128)(2,1)S(1)} %copy-done.5, bf16[1,9,256,8,128]{2,4,1,3,0:T(8,128)(2,1)} %copy-done.11), kind=kOutput, calls=%fused_computation.55 | convolution fusion | flops 1210843136 | bytes 7995392 | tf_op jit(solution)/shard_map/toc,btchw->bohw/dot_general | solution.py:65
  94.9 2.9 fusion.8
  97.8 3.0 collective-permute-start.6
  101.1 3.7 collective-permute-done.6
  111.6 2.9 fusion.11
  114.9 3.3 fusion.29
  118.3 7.1 %scatter-add.110 = f32[1,256,10,130]{1,3,2,0:T(8,128)S(1)} dynamic-update-slice(f32[1,256,10,130]{1,3,2,0:T(8,128)S(1)} %scatter-add.109, f32[1,256,8,128]{1,3,2,0:T(8,128)} %fusion.29, s32[]{:T(128)} %constant.657.clone.1, s32[]{:T(128)} %constant.657.clone.1, s32[]{:T(128)} %bitcast.51, s32[]{:T(128)} %bitcast.52) | dynamic-update-slice | bytes 2097156 | tf_op jit(solution)/shard_map/scatter-add | solution.py:81
  125.4 4.1 %add_select_fusion = f32[1,256,8,128]{1,3,2,0:T(8,128)} fusion(f32[1,256,10,130]{1,3,2,0:T(8,128)S(1)} %scatter-add.110, s32[]{:T(128)} %bitcast.57, s32[]{:T(128)} %bitcast.58, bf16[1,256,8,128]{1,3,2,0:T(8,128)(2,1)S(1)} %get-tuple-element.336, pred[]{:T(512)} %and_reduce_fusion, bf16[9,256,256]{2,1,0:T(8,128)(2,1)} %param.58), kind=kOutput, calls=%fused_computation.10 | convolution fusion | flops 134742016 | bytes 2754048 | tf_op jit(solution)/shard_map/oc,bohw->bchw/dot_general | solution.py:73
  129.5 7.2 %scatter-add.111 = f32[1,256,10,130]{1,3,2,0:T(8,128)S(1)} dynamic-update-slice(f32[1,256,10,130]{1,3,2,0:T(8,128)S(1)} %scatter-add.110, f32[1,256,8,128]{1,3,2,0:T(8,128)} %add_select_fusion, s32[]{:T(128)} %constant.657.clone.1, s32[]{:T(128)} %constant.657.clone.1, s32[]{:T(128)} %bitcast.57, s32[]{:T(128)} %bitcast.58) | dynamic-update-slice | bytes 2097156 | tf_op jit(solution)/shard_map/scatter-add | solution.py:81
  140.1 5.9 %scatter-add.115 = f32[1,256,10,130]{1,3,2,0:T(8,128)S(1)} dynamic-update-slice(f32[1,256,10,130]{1,3,2,0:T(8,128)S(1)} %fusion.31, f32[1,256,8,128]{1,3,2,0:T(8,128)} %fusion.32, s32[]{:T(128)} %constant.657.clone.1, s32[]{:T(128)} %constant.657.clone.1, s32[]{:T(128)} %constant.670.clone.1, s32[]{:T(128)} %constant.670.clone.1) | dynamic-update-slice | bytes 2097156 | tf_op jit(solution)/shard_map/scatter-add | solution.py:81
  148.1 5.9 %scatter-add.116 = f32[1,256,10,130]{1,3,2,0:T(8,128)S(1)} dynamic-update-slice(f32[1,256,10,130]{1,3,2,0:T(8,128)S(1)} %scatter-add.115, f32[1,256,8,128]{1,3,2,0:T(8,128)} %fusion.33, s32[]{:T(128)} %constant.657.clone.1, s32[]{:T(128)} %constant.657.clone.1, s32[]{:T(128)} %constant.670.clone.1, s32[]{:T(128)} %constant.667.clone.1) | dynamic-update-slice | bytes 2097156 | tf_op jit(solution)/shard_map/scatter-add | solution.py:81
  157.4 5.9 %scatter-add.120 = f32[1,256,10,130]{1,3,2,0:T(8,128)S(1)} dynamic-update-slice(f32[1,256,10,130]{1,3,2,0:T(8,128)S(1)} %fusion.35, f32[1,256,8,128]{1,3,2,0:T(8,128)} %fusion.36, s32[]{:T(128)} %constant.657.clone.1, s32[]{:T(128)} %constant.657.clone.1, s32[]{:T(128)} %constant.667.clone.1, s32[]{:T(128)} %constant.670.clone.1) | dynamic-update-slice | bytes 2097156 | tf_op jit(solution)/shard_map/scatter-add | solution.py:81
  165.5 5.9 %scatter-add.121 = f32[1,256,10,130]{1,3,2,0:T(8,128)S(1)} dynamic-update-slice(f32[1,256,10,130]{1,3,2,0:T(8,128)S(1)} %scatter-add.120, f32[1,256,8,128]{1,3,2,0:T(8,128)} %fusion.37, s32[]{:T(128)} %constant.657.clone.1, s32[]{:T(128)} %constant.657.clone.1, s32[]{:T(128)} %constant.667.clone.1, s32[]{:T(128)} %constant.667.clone.1) | dynamic-update-slice | bytes 2097156 | tf_op jit(solution)/shard_map/scatter-add | solution.py:81
  171.3 62.5 %all-reduce.9.cloned.1.call-done = (f32[9,256,256]{1,2,0:T(8,128)}, f32[9,256,256]{1,2,0:T(8,128)}) async-done(((f32[9,256,256]{1,2,0:T(8,128)}, f32[9,256,256]{1,2,0:T(8,128)}), (f32[9,256,256]{1,2,0:T(8,128)}, f32[9,256,256]{1,2,0:T(8,128)})) %all-reduce.9.cloned.1.call-update) | async-done | bytes 4718608 | tf_op jit(solution)/shard_map/psum | solution.py:119
  235.2 4.9 %collective-permute-start.12 = (f32[1,256,1,130]{1,3,2,0:T(8,128)}, f32[1,256,1,130]{1,3,2,0:T(8,128)S(1)}, u32[]{:S(2)}, u32[]{:S(2)}) collective-permute-start(f32[1,256,1,130]{1,3,2,0:T(8,128)} %get-tuple-element.325), channel_id=1, source_target_pairs={{0,4},{4,8},{8,12},{12,16},{16,20},{20,24},{24,28},{1,5},{5,9},{9,... | collective-permute-start | bytes 399368 | tf_op jit(solution)/shard_map/ppermute | solution.py:15
  242.3 5.6 %collective-permute-done.13 = f32[1,256,1,130]{1,3,2,0:T(8,128)S(1)} collective-permute-done((f32[1,256,1,130]{1,3,2,0:T(8,128)S(1)}, f32[1,256,1,130]{1,3,2,0:T(8,128)S(1)}, u32[]{:S(2)}, u32[]{:S(2)}) %collective-permute-start.13) | collective-permute-done | bytes 133152 | tf_op jit(solution)/shard_map/ppermute | solution.py:17
  249.4 3.8 %fusion.41 = bf16[1,256,8,128]{1,3,2,0:T(8,128)(2,1)S(1)} fusion(bf16[1,9,256,8,128]{2,4,3,1,0:T(8,128)(2,1)} %copy-done.13, bf16[9,256,256]{2,1,0:T(8,128)(2,1)S(1)} %copy-done.6, bf16[1,256,8,128]{1,3,2,0:T(8,128)(2,1)S(1)} %copy.9), kind=kOutput, calls=%fused_computation.51 | convolution fusion | flops 1208745984 | bytes 6946816 | tf_op jit(solution)/shard_map/toc,btchw->bohw/dot_general | solution.py:65
  255.8 2.8 collective-permute-done.15
  259.9 99.3 %all-reduce.7.cloned.1.call-done = (f32[9,256,256]{1,2,0:T(8,128)}, f32[9,256,256]{1,2,0:T(8,128)}) async-done(((f32[9,256,256]{1,2,0:T(8,128)}, f32[9,256,256]{1,2,0:T(8,128)}), (f32[9,256,256]{1,2,0:T(8,128)}, f32[9,256,256]{1,2,0:T(8,128)})) %all-reduce.7.cloned.1.call-update) | async-done | bytes 4718608 | tf_op jit(solution)/shard_map/psum | solution.py:119
  359.2 3.2 copy.38
  (145 shorter events, 66.4 us)
Async XLA Ops:
  7.2 7.0 %copy-start = (bf16[1,256,8,128]{3,2,1,0:T(8,128)(2,1)S(1)}, bf16[1,256,8,128]{3,2,1,0:T(8,128)(2,1)}, u32[]{:S(2)}) copy-start(bf16[1,256,8,128]{3,2,1,0:T(8,128)(2,1)} %param.61) | copy-start | bytes 1572868
  7.2 226.6 %all-reduce.9.cloned.1.call-start = ((), (), s32[]{:S(2)}) async-start(), calls=%async_computation.1 | async-start | bytes 9437184 | tf_op jit(solution)/shard_map/psum | solution.py:119
  8.6 42.3 %collective-permute-start = (bf16[1,256,8,1]{1,3,2,0:T(2,128)(2,1)S(1)}, bf16[1,256,8,1]{1,3,2,0:T(2,128)(2,1)S(1)}, u32[]{:S(2)}, u32[]{:S(2)}) collective-permute-start(bf16[1,256,8,1]{1,3,2,0:T(2,128)(2,1)S(1)} %get-tuple-element.348), channel_id=1, source_target_pairs={{0,32},{32,64},{64,96},{96,128},{128,160},{160,192},{192,224},{224... | collective-permute-start | bytes 12296 | tf_op jit(solution)/shard_map/ppermute | solution.py:15
  11.5 39.3 %collective-permute-start.1 = (bf16[1,256,8,1]{1,3,2,0:T(2,128)(2,1)S(1)}, bf16[1,256,8,1]{1,3,2,0:T(2,128)(2,1)S(1)}, u32[]{:S(2)}, u32[]{:S(2)}) collective-permute-start(bf16[1,256,8,1]{1,3,2,0:T(2,128)(2,1)S(1)} %get-tuple-element.349), channel_id=1, source_target_pairs={{32,0},{64,32},{96,64},{128,96},{160,128},{192,160},{224,192},{0,2... | collective-permute-start | bytes 12296 | tf_op jit(solution)/shard_map/ppermute | solution.py:17
  50.9 13.1 %collective-permute-start.3 = (bf16[1,256,1,130]{1,3,2,0:T(8,128)(2,1)S(1)}, bf16[1,256,1,130]{1,3,2,0:T(8,128)(2,1)S(1)}, u32[]{:S(2)}, u32[]{:S(2)}) collective-permute-start(bf16[1,256,1,130]{1,3,2,0:T(8,128)(2,1)S(1)} %get-tuple-element.344), channel_id=1, source_target_pairs={{4,0},{8,4},{12,8},{16,12},{20,16},{24,20},{28,24},{0,28},{5,1},{9... | collective-permute-start | bytes 199688 | tf_op jit(solution)/shard_map/ppermute | solution.py:17
  56.2 17.0 %collective-permute-start.9 = (f32[1,256,1,130]{1,3,2,0:T(8,128)S(1)}, f32[1,256,1,130]{1,3,2,0:T(8,128)S(1)}, u32[]{:S(2)}, u32[]{:S(2)}) collective-permute-start(f32[1,256,1,130]{1,3,2,0:T(8,128)S(1)} %get-tuple-element.328), channel_id=1, source_target_pairs={{4,0},{8,4},{12,8},{16,12},{20,16},{24,20},{28,24},{5,1},{9,5},{13... | collective-permute-start | bytes 399368 | tf_op jit(solution)/shard_map/ppermute | solution.py:17
  57.5 14.8 %collective-permute-start.8 = (f32[1,256,1,130]{1,3,2,0:T(8,128)S(1)}, f32[1,256,1,130]{1,3,2,0:T(8,128)S(1)}, u32[]{:S(2)}, u32[]{:S(2)}) collective-permute-start(f32[1,256,1,130]{1,3,2,0:T(8,128)S(1)} %get-tuple-element.329), channel_id=1, source_target_pairs={{0,4},{4,8},{8,12},{12,16},{16,20},{20,24},{24,28},{1,5},{5,9},{9,... | collective-permute-start | bytes 399368 | tf_op jit(solution)/shard_map/ppermute | solution.py:15
  64.1 6.8 %collective-permute-start.2 = (bf16[1,256,1,130]{1,3,2,0:T(8,128)(2,1)S(1)}, bf16[1,256,1,130]{1,3,2,0:T(8,128)(2,1)S(1)}, u32[]{:S(2)}, u32[]{:S(2)}) collective-permute-start(bf16[1,256,1,130]{1,3,2,0:T(8,128)(2,1)S(1)} %get-tuple-element.345), channel_id=1, source_target_pairs={{0,4},{4,8},{8,12},{12,16},{16,20},{20,24},{24,28},{28,0},{1,5},{5... | collective-permute-start | bytes 199688 | tf_op jit(solution)/shard_map/ppermute | solution.py:15
  71.9 1.3 copy-start.1
  73.3 12.2 %copy-start.5 = (bf16[9,256,256]{2,1,0:T(8,128)(2,1)S(1)}, bf16[9,256,256]{2,1,0:T(8,128)(2,1)}, u32[]{:S(2)}) copy-start(bf16[9,256,256]{2,1,0:T(8,128)(2,1)} %param.58) | copy-start | bytes 3538948
  73.3 6.1 %collective-permute-start.10 = (f32[1,256,8,1]{1,3,2,0:T(1,128)S(1)}, f32[1,256,8,1]{1,3,2,0:T(1,128)S(1)}, u32[]{:S(2)}, u32[]{:S(2)}) collective-permute-start(f32[1,256,8,1]{1,3,2,0:T(1,128)S(1)} %get-tuple-element.335), channel_id=1, source_target_pairs={{0,32},{32,64},{64,96},{96,128},{128,160},{160,192},{192,224},{224... | collective-permute-start | bytes 24584 | tf_op jit(solution)/shard_map/ppermute | solution.py:15
  76.2 2.2 copy-start.11
  79.4 3.7 %collective-permute-start.11 = (f32[1,256,8,1]{1,3,2,0:T(1,128)S(1)}, f32[1,256,8,1]{1,3,2,0:T(1,128)S(1)}, u32[]{:S(2)}, u32[]{:S(2)}) collective-permute-start(f32[1,256,8,1]{1,3,2,0:T(1,128)S(1)} %get-tuple-element.334), channel_id=1, source_target_pairs={{32,0},{64,32},{96,64},{128,96},{160,128},{192,160},{224,192},{0,2... | collective-permute-start | bytes 24584 | tf_op jit(solution)/shard_map/ppermute | solution.py:17
  85.5 9.4 %copy-start.12 = (bf16[1,9,256,8,128]{2,4,1,3,0:T(8,128)(2,1)S(1)}, bf16[1,9,256,8,128]{2,4,1,3,0:T(8,128)(2,1)}, u32[]{:S(2)}) copy-start(bf16[1,9,256,8,128]{2,4,1,3,0:T(8,128)(2,1)} %copy-done.11) | copy-start | bytes 14155780
  89.9 2.6 collective-permute-start.4
  90.5 3.7 %collective-permute-start.5 = (bf16[1,256,8,1]{1,3,2,0:T(2,128)(2,1)S(1)}, bf16[1,256,8,1]{1,3,2,0:T(2,128)(2,1)S(1)}, u32[]{:S(2)}, u32[]{:S(2)}) collective-permute-start(bf16[1,256,8,1]{1,3,2,0:T(2,128)(2,1)S(1)} %get-tuple-element.347), channel_id=1, source_target_pairs={{32,0},{64,32},{96,64},{128,96},{160,128},{192,160},{224,192},{0,2... | collective-permute-start | bytes 12296 | tf_op jit(solution)/shard_map/ppermute | solution.py:17
  92.5 2.4 copy-start.9
  94.2 0.7 copy-start.7
  94.9 5.9 %collective-permute-start.7 = (bf16[1,256,1,130]{1,3,2,0:T(8,128)(2,1)S(1)}, bf16[1,256,1,130]{1,3,2,0:T(8,128)(2,1)S(1)}, u32[]{:S(2)}, u32[]{:S(2)}) collective-permute-start(bf16[1,256,1,130]{1,3,2,0:T(8,128)(2,1)S(1)} %get-tuple-element.340), channel_id=1, source_target_pairs={{4,0},{8,4},{12,8},{16,12},{20,16},{24,20},{28,24},{0,28},{5,1},{9... | collective-permute-start | bytes 199688 | tf_op jit(solution)/shard_map/ppermute | solution.py:17
  97.8 7.0 %collective-permute-start.6 = (bf16[1,256,1,130]{1,3,2,0:T(8,128)(2,1)}, bf16[1,256,1,130]{1,3,2,0:T(8,128)(2,1)S(1)}, u32[]{:S(2)}, u32[]{:S(2)}) collective-permute-start(bf16[1,256,1,130]{1,3,2,0:T(8,128)(2,1)} %get-tuple-element.341), channel_id=1, source_target_pairs={{0,4},{4,8},{8,12},{12,16},{16,20},{20,24},{24,28},{28,0},{1,5},{5... | collective-permute-start | bytes 199688 | tf_op jit(solution)/shard_map/ppermute | solution.py:15
  108.1 0.7 copy-start.10
  108.3 0.7 copy-start.8
  109.4 2.2 copy-start.13
  114.5 244.7 %all-reduce.7.cloned.1.call-start = ((), (), s32[]{:S(2)}) async-start(), calls=%async_computation | async-start | bytes 9437184 | tf_op jit(solution)/shard_map/psum | solution.py:119
  235.2 7.1 %collective-permute-start.12 = (f32[1,256,1,130]{1,3,2,0:T(8,128)}, f32[1,256,1,130]{1,3,2,0:T(8,128)S(1)}, u32[]{:S(2)}, u32[]{:S(2)}) collective-permute-start(f32[1,256,1,130]{1,3,2,0:T(8,128)} %get-tuple-element.325), channel_id=1, source_target_pairs={{0,4},{4,8},{8,12},{12,16},{16,20},{20,24},{24,28},{1,5},{5,9},{9,... | collective-permute-start | bytes 399368 | tf_op jit(solution)/shard_map/ppermute | solution.py:15
  240.3 9.0 %copy-start.6 = (bf16[9,256,256]{2,1,0:T(8,128)(2,1)S(1)}, bf16[9,256,256]{2,1,0:T(8,128)(2,1)}, u32[]{:S(2)}) copy-start(bf16[9,256,256]{2,1,0:T(8,128)(2,1)} %param.59) | copy-start | bytes 3538948
  240.4 7.4 %collective-permute-start.13 = (f32[1,256,1,130]{1,3,2,0:T(8,128)S(1)}, f32[1,256,1,130]{1,3,2,0:T(8,128)S(1)}, u32[]{:S(2)}, u32[]{:S(2)}) collective-permute-start(f32[1,256,1,130]{1,3,2,0:T(8,128)S(1)} %get-tuple-element.324), channel_id=1, source_target_pairs={{4,0},{8,4},{12,8},{16,12},{20,16},{24,20},{28,24},{5,1},{9,5},{13... | collective-permute-start | bytes 399368 | tf_op jit(solution)/shard_map/ppermute | solution.py:17
  247.9 1.0 copy-start.2
  248.9 6.8 %collective-permute-start.14 = (f32[1,256,8,1]{1,3,2,0:T(1,128)S(1)}, f32[1,256,8,1]{1,3,2,0:T(1,128)S(1)}, u32[]{:S(2)}, u32[]{:S(2)}) collective-permute-start(f32[1,256,8,1]{1,3,2,0:T(1,128)S(1)} %get-tuple-element.333), channel_id=1, source_target_pairs={{0,32},{32,64},{64,96},{96,128},{128,160},{160,192},{192,224},{224... | collective-permute-start | bytes 24584 | tf_op jit(solution)/shard_map/ppermute | solution.py:15
  249.4 4.9 %copy-start.3 = (f32[1,256,8,130]{1,3,2,0:T(8,128)S(1)}, f32[1,256,8,130]{1,3,2,0:T(8,128)}, u32[]{:S(2)}) copy-start(f32[1,256,8,130]{1,3,2,0:T(8,128)} %copy-done.2) | copy-start | bytes 3194884
  254.4 4.2 %collective-permute-start.15 = (f32[1,256,8,1]{1,3,2,0:T(1,128)S(1)}, f32[1,256,8,1]{1,3,2,0:T(1,128)S(1)}, u32[]{:S(2)}, u32[]{:S(2)}) collective-permute-start(f32[1,256,8,1]{1,3,2,0:T(1,128)S(1)} %get-tuple-element.332), channel_id=1, source_target_pairs={{32,0},{64,32},{96,64},{128,96},{160,128},{192,160},{224,192},{0,2... | collective-permute-start | bytes 24584 | tf_op jit(solution)/shard_map/ppermute | solution.py:17
  359.2 3.2 copy-start.4
Sparse Core Ops, SparseCore 0:
  114.6 119.1 all-reduce.8
  237.2 121.9 all-reduce.6
